TPU v7x, 512 devices: a whole 4x8x8 slice. The times are simulated.
512 devices in a mesh: dp: 16 (over y, core), ctx: 32 (over z, x).
Axes of the slice: x: 4, y: 8, z: 8, core: 2. Of those that a mesh axis runs over, the one named last changes fastest.
Arguments:
- queries: bfloat16 [16, 4096, 4096], P('dp', 'ctx'), may hold values from -9 to 9
- keys: bfloat16 [16, 4096, 1024], P('dp', 'ctx'), may hold values from -9 to 9
- values: bfloat16 [16, 4096, 1024], P('dp', 'ctx'), may hold values from -6 to 6
- doc_lengths: int32 [16, 128], P('dp'), may hold values from 1 to 128, as said below
- cotangent: float32 [16, 128, 4096], P('dp', 'ctx'), may hold values from -50 to 50
- query_gain: float32 [128], replicated, may hold values from 0.6 to 4.5
- key_gain: float32 [128], replicated, may hold values from 0.6 to 4.5
Outputs:
- embed_quarter: float32 [16, 128, 1024], P('dp', 'ctx')
- embed_half: float32 [16, 128, 2048], P('dp', 'ctx')
- embed_full: float32 [16, 128, 4096], P('dp', 'ctx')
- grad_queries: bfloat16 [16, 4096, 4096], P('dp', 'ctx')
- grad_keys: bfloat16 [16, 4096, 1024], P('dp', 'ctx')
- grad_values: bfloat16 [16, 4096, 1024], P('dp', 'ctx')
- grad_query_gain: float32 [128], replicated
- grad_key_gain: float32 [128], replicated
Inputs may be any that keep to these rules, and one draw needn't show every extreme that they name: `doc_lengths`: each sequence's 128 lengths sum to 4096; the first of them is exactly 128. The last 65 documents of each sequence together span at most 128 tokens.
All inputs are finite; a program needn't handle non-finite values.
Results may differ from a plain program's by a relative error of at most 0.0054.
The roundings to bfloat16 on the way count: a program that leaves them out, or rounds other values in their place, can miss the bound.
Values may be sent and summed in bfloat16 or wider, within the bound.
A program may use at most 64 MiB of HBM per device.

v0:
```python
import math
import jax
import jax.numpy as jnp
from jax import lax
from jax.sharding import PartitionSpec as P

EPS = 1e-06


def rms_forward(field, gain):
    inverse = lax.rsqrt(jnp.mean(field * field, axis=-1, keepdims=True) + EPS)
    unit = field * inverse
    return (unit * gain, unit, inverse)


def rms_backward(grad, unit, inverse, gain):
    scaled = grad * gain
    inner = jnp.mean(scaled * unit, axis=-1, keepdims=True)
    grad_in = inverse * (scaled - unit * inner)
    grad_gain = jnp.sum((grad * unit).reshape(-1, unit.shape[-1]), axis=0)
    return (grad_in, grad_gain)


def doc_ids(lengths, positions, total):
    ends = jnp.cumsum(lengths, dtype=jnp.int32)
    owner = jnp.sum((positions[:, None] >= ends[None, :]).astype(jnp.int32), axis=1)
    inside = (positions >= 0) & (positions < total)
    return jnp.where(inside, owner, -1)


def block_probs(queries, keys, query_ids, key_ids):
    rows, heads, width = queries.shape
    query_groups = keys.shape[1]
    grouped = queries.reshape(rows, query_groups, heads // query_groups, width)
    scores = jnp.einsum("rgpe,kge->gprk", grouped, keys, preferred_element_type=jnp.float32) * (
        1.0 / math.sqrt(width)
    )
    allowed = query_ids[:, None] == key_ids[None, :]
    scores = jnp.where(allowed[None, None], scores, -jnp.inf)
    top = jnp.max(scores, axis=-1, keepdims=True)
    powers = jnp.exp(scores - top)
    return (powers / jnp.sum(powers, axis=-1, keepdims=True), grouped)


def forward_block(queries, keys, values, query_ids, key_ids):
    probs, grouped = block_probs(queries, keys, query_ids, key_ids)
    low = probs.astype(jnp.bfloat16)
    mixed = jnp.einsum("gprk,kge->rgpe", low, values, preferred_element_type=jnp.float32)
    return mixed.reshape(queries.shape[0], -1).astype(jnp.bfloat16)


def backward_block(queries, keys, values, query_ids, key_ids, grad_out):
    probs, grouped = block_probs(queries, keys, query_ids, key_ids)
    low = probs.astype(jnp.bfloat16)
    rows, heads, width = queries.shape
    query_groups = keys.shape[1]
    grad_four = grad_out.reshape(rows, query_groups, heads // query_groups, width)
    grad_probs = jnp.einsum("rgpe,kge->gprk", grad_four, values, preferred_element_type=jnp.float32)
    inner = jnp.sum(probs * grad_probs, axis=-1, keepdims=True)
    grad_scores = (probs * (grad_probs - inner)).astype(jnp.bfloat16)
    scale = 1.0 / math.sqrt(width)
    grad_q = (
        jnp.einsum("gprk,kge->rgpe", grad_scores, keys, preferred_element_type=jnp.float32) * scale
    )
    grad_k = (
        jnp.einsum("gprk,rgpe->kge", grad_scores, grouped, preferred_element_type=jnp.float32)
        * scale
    )
    grad_v = jnp.einsum("gprk,rgpe->kge", low, grad_four, preferred_element_type=jnp.float32)
    return (grad_q.reshape(rows, heads, width), grad_k, grad_v)


def band_setup(keys, values, lengths, margin, total):
    key_pad = jnp.pad(keys, ((margin, margin), (0, 0), (0, 0)))
    value_pad = jnp.pad(values, ((margin, margin), (0, 0), (0, 0)))
    pad_ids = doc_ids(lengths, jnp.arange(total + 2 * margin, dtype=jnp.int32) - margin, total)
    return (key_pad, value_pad, pad_ids)


def band_forward(normed, padded, token_ids, margin):
    key_pad, value_pad, pad_ids = padded
    total = normed.shape[0]
    block = min(512, 4 * margin)
    window = block + 2 * margin

    def forward(index):
        start = index * block
        return forward_block(
            lax.dynamic_slice_in_dim(normed, start, block, 0),
            lax.dynamic_slice_in_dim(key_pad, start, window, 0),
            lax.dynamic_slice_in_dim(value_pad, start, window, 0),
            lax.dynamic_slice_in_dim(token_ids, start, block, 0),
            lax.dynamic_slice_in_dim(pad_ids, start, window, 0),
        )

    return lax.map(forward, jnp.arange(total // block, dtype=jnp.int32)).reshape(total, -1)


def band_backward(normed, padded, token_ids, margin, grad_out):
    key_pad, value_pad, pad_ids = padded
    total, heads, width = normed.shape
    block = min(512, 4 * margin)
    window = block + 2 * margin
    zeros = jnp.zeros(key_pad.shape, jnp.float32)

    def backward(carry, index):
        key_acc, value_acc = carry
        start = index * block
        grad_q, grad_k, grad_v = backward_block(
            lax.dynamic_slice_in_dim(normed, start, block, 0),
            lax.dynamic_slice_in_dim(key_pad, start, window, 0),
            lax.dynamic_slice_in_dim(value_pad, start, window, 0),
            lax.dynamic_slice_in_dim(token_ids, start, block, 0),
            lax.dynamic_slice_in_dim(pad_ids, start, window, 0),
            lax.dynamic_slice_in_dim(grad_out, start, block, 0),
        )
        key_acc = lax.dynamic_update_slice_in_dim(
            key_acc, lax.dynamic_slice_in_dim(key_acc, start, window, 0) + grad_k, start, 0
        )
        value_acc = lax.dynamic_update_slice_in_dim(
            value_acc, lax.dynamic_slice_in_dim(value_acc, start, window, 0) + grad_v, start, 0
        )
        return ((key_acc, value_acc), grad_q)

    (key_acc, value_acc), grad_blocks = lax.scan(
        backward, (zeros, zeros), jnp.arange(total // block, dtype=jnp.int32)
    )
    return (
        grad_blocks.reshape(total, heads, width),
        key_acc[margin : margin + total],
        value_acc[margin : margin + total],
    )


def matryoshka(pooled, cotangent):
    width = pooled.shape[-1]
    prefixes = (width // 4, width // 2, width)

    def embed(field):
        return tuple(
            (
                field[:, :count]
                * lax.rsqrt(
                    jnp.sum(field[:, :count] * field[:, :count], axis=-1, keepdims=True) + EPS
                )
                for count in prefixes
            )
        )

    embeds, pullback = jax.vjp(embed, pooled)
    (grad,) = pullback(tuple((cotangent[:, :count] for count in prefixes)))
    return (embeds, grad)


def pool_tokens(attended, token_ids, docs, own_lengths):
    onehot = (token_ids[:, None] == jnp.arange(docs, dtype=jnp.int32)[None, :]).astype(jnp.bfloat16)
    partial_sums = jnp.dot(onehot.T, attended, preferred_element_type=jnp.float32)
    return lax.psum_scatter(partial_sums, "ctx", scatter_dimension=0, tiled=True) / own_lengths


def spread_tokens(scaled, token_ids):
    whole = lax.all_gather(scaled.astype(jnp.bfloat16), "ctx", axis=0, tiled=True).astype(
        scaled.dtype
    )
    return jnp.take(whole, token_ids, axis=0).astype(jnp.bfloat16)


def body(queries, keys, values, doc_lengths, cotangent, query_gain, key_gain):
    rows = queries.shape[1]
    model = queries.shape[2]
    width = query_gain.shape[0]
    heads = model // width
    kv_width = keys.shape[2]
    query_groups = kv_width // width
    group_repeat = heads // query_groups
    shards = lax.axis_size("ctx")
    position = lax.axis_index("ctx")
    total = rows * shards
    lengths = doc_lengths[0]
    docs = lengths.shape[0]
    owned = docs // shards
    own_ids = doc_ids(lengths, position * rows + jnp.arange(rows, dtype=jnp.int32), total)
    own_lengths = lax.dynamic_slice_in_dim(lengths, position * owned, owned).astype(jnp.float32)[
        :, None
    ]
    normed_kf, unit_k, inv_k = rms_forward(
        keys[0].astype(jnp.float32).reshape(rows, query_groups, width), key_gain
    )
    normed_k = normed_kf.astype(jnp.bfloat16)
    key_rep = jnp.repeat(normed_k, group_repeat, axis=1).reshape(rows, model)
    value_rep = jnp.repeat(
        values[0].reshape(rows, query_groups, width), group_repeat, axis=1
    ).reshape(rows, model)
    head_q, head_k, head_v = (
        lax.all_to_all(queries[0], "ctx", split_axis=1, concat_axis=0, tiled=True),
        lax.all_to_all(key_rep, "ctx", split_axis=1, concat_axis=0, tiled=True),
        lax.all_to_all(value_rep, "ctx", split_axis=1, concat_axis=0, tiled=True),
    )
    local_heads = model // shards // width
    normed_qf, unit_q, inv_q = rms_forward(
        head_q.astype(jnp.float32).reshape(total, local_heads, width), query_gain
    )
    normed_q = normed_qf.astype(jnp.bfloat16)
    all_ids = doc_ids(lengths, jnp.arange(total, dtype=jnp.int32), total)
    padded = band_setup(
        head_k.reshape(total, local_heads, width),
        head_v.reshape(total, local_heads, width),
        lengths,
        rows,
        total,
    )
    attended = band_forward(normed_q, padded, all_ids, rows)
    back_rows = lax.all_to_all(attended, "ctx", split_axis=0, concat_axis=1, tiled=True)
    pooled = pool_tokens(back_rows, own_ids, docs, own_lengths)
    embeds, grad_pooled = matryoshka(pooled, cotangent[0])
    grad_rows = spread_tokens(grad_pooled / own_lengths, own_ids)
    grad_out = lax.all_to_all(grad_rows, "ctx", split_axis=1, concat_axis=0, tiled=True)
    grad_nq, grad_head_k, grad_head_v = band_backward(normed_q, padded, all_ids, rows, grad_out)
    grad_qf, grad_qgain = rms_backward(grad_nq, unit_q, inv_q, query_gain)
    grad_q = lax.all_to_all(
        grad_qf.astype(jnp.bfloat16).reshape(total, local_heads * width),
        "ctx",
        split_axis=0,
        concat_axis=1,
        tiled=True,
    )
    share_k, share_v = (
        lax.all_to_all(
            grad_head_k.reshape(total, local_heads * width),
            "ctx",
            split_axis=0,
            concat_axis=1,
            tiled=True,
        ),
        lax.all_to_all(
            grad_head_v.reshape(total, local_heads * width),
            "ctx",
            split_axis=0,
            concat_axis=1,
            tiled=True,
        ),
    )
    grad_nk = jnp.sum(share_k.reshape(rows, query_groups, group_repeat, width), axis=2)
    grad_vf = jnp.sum(share_v.reshape(rows, query_groups, group_repeat, width), axis=2)
    grad_kf, grad_kgain = rms_backward(grad_nk, unit_k, inv_k, key_gain)
    total_qgain, total_kgain = lax.psum((grad_qgain, grad_kgain), ("dp", "ctx"))
    return (
        embeds[0][None],
        embeds[1][None],
        embeds[2][None],
        grad_q[None],
        grad_kf.astype(jnp.bfloat16).reshape(rows, kv_width)[None],
        grad_vf.astype(jnp.bfloat16).reshape(rows, kv_width)[None],
        total_qgain,
        total_kgain,
    )


def solution(mesh):
    in_specs = (
        P("dp", "ctx", None),
        P("dp", "ctx", None),
        P("dp", "ctx", None),
        P("dp", None),
        P("dp", "ctx", None),
        P(),
        P(),
    )
    out_specs = (
        P("dp", "ctx", None),
        P("dp", "ctx", None),
        P("dp", "ctx", None),
        P("dp", "ctx", None),
        P("dp", "ctx", None),
        P("dp", "ctx", None),
        P(),
        P(),
    )
    return jax.shard_map(body, mesh=mesh, in_specs=in_specs, out_specs=out_specs, check_vma=False)
```

profile of v0, /device:TPU:1, one launch (start us, length us, event | category | flops | bytes accessed | tf_op | source)
XLA Modules:
  0.0 838.3 jit_solution(9058164657707362389)
XLA Ops:
  9.4 13.7 %all-to-all-start = ((bf16[128,32,128]{2,0,1:T(8,128)(2,1)}), bf16[128,32,128]{2,0,1:T(8,128)(2,1)S(1)}, u32[]{:S(2)}, u32[]{:S(2)}) async-start(bf16[128,32,128]{2,0,1:T(8,128)(2,1)} %bitcast.29), calls=%async_computation | async-start | bytes 2097152 | tf_op jit(solution)/shard_map/all_to_all | solution.py:197
  24.8 24.6 %all-to-all-done = bf16[128,32,128]{2,0,1:T(8,128)(2,1)S(1)} async-done(((bf16[128,32,128]{2,0,1:T(8,128)(2,1)}), bf16[128,32,128]{2,0,1:T(8,128)(2,1)S(1)}, u32[]{:S(2)}, u32[]{:S(2)}) %all-to-all-start) | async-done | bytes 1048608 | tf_op jit(solution)/shard_map/all_to_all | solution.py:197
  50.6 6.4 all-to-all-start.1
  59.3 23.0 %all-to-all-done.1 = bf16[128,32,128]{2,0,1:T(8,128)(2,1)S(1)} async-done(((bf16[128,32,128]{2,0,1:T(8,128)(2,1)}), bf16[128,32,128]{2,0,1:T(8,128)(2,1)S(1)}, u32[]{:S(2)}, u32[]{:S(2)}) %all-to-all-start.1) | async-done | bytes 1048608 | tf_op jit(solution)/shard_map/all_to_all | solution.py:196
  82.2 6.8 all-to-all-start.2
  95.0 18.5 %all-to-all-done.2 = bf16[128,32,128]{0,2,1:T(8,128)(2,1)S(1)} async-done(((bf16[128,32,128]{0,2,1:T(8,128)(2,1)}), bf16[128,32,128]{0,2,1:T(8,128)(2,1)S(1)}, u32[]{:S(2)}, u32[]{:S(2)}) %all-to-all-start.2) | async-done | bytes 1048608 | tf_op jit(solution)/shard_map/all_to_all | solution.py:195
  119.0 41.8 %while.24 = (s32[]{:T(128)}, bf16[8,512,128]{2,1,0:T(8,128)(2,1)}, s32[8]{0:T(128)S(1)}, bf16[4352,1,128]{2,0,1:T(8,128)(2,1)}, s32[4096]{0:T(1024)S(1)}, /*inde...) while((s32[]{:T(128)}, bf16[8,512,128]{2,1,0:T(8,128)(2,1)}, ...), condition=%wide.region_9.10_spmd, body=%wide.region_6.9_spmd.sunk | while | flops 204930048 | bytes 5924080 | solution.py:96
  160.9 7.4 all-to-all-start.3
  168.5 24.6 %all-to-all-done.3 = bf16[32,128,128]{2,1,0:T(8,128)(2,1)S(1)} async-done(((bf16[32,128,128]{2,1,0:T(8,128)(2,1)}), bf16[32,128,128]{2,1,0:T(8,128)(2,1)S(1)}, u32[]{:S(2)}, u32[]{:S(2)}) %all-to-all-start.3) | async-done | bytes 1048608 | tf_op jit(solution)/shard_map/all_to_all | solution.py:213
  197.7 160.3 %all-reduce.10.cloned.1.call-done = f32[128,4096]{1,0:T(8,128)} async-done(((f32[128,4096]{1,0:T(8,128)}), f32[128,4096]{1,0:T(8,128)}) %all-reduce.10.cloned.1.call-update) | async-done | bytes 2097168
  361.7 79.2 %all-gather.3.cloned.1.call-done = bf16[32,4,4096]{2,1,0:T(4,128)(2,1)} async-done(((bf16[1,4,4096]{2,1,0:T(4,128)(2,1)}), bf16[32,4,4096]{2,1,0:T(4,128)(2,1)}) %all-gather.3.cloned.1.call-update) | async-done | bytes 1048592 | tf_op jit(solution)/shard_map/all_gather | solution.py:162
  444.8 5.9 all-to-all-start.4
  451.4 21.0 %all-to-all-done.4 = bf16[128,32,128]{2,0,1:T(8,128)(2,1)} async-done(((bf16[128,32,128]{2,0,1:T(8,128)(2,1)}), bf16[128,32,128]{2,0,1:T(8,128)(2,1)}, u32[]{:S(2)}, u32[]{:S(2)}) %all-to-all-start.4) | async-done | bytes 1048608 | tf_op jit(solution)/shard_map/all_to_all | solution.py:217
  475.4 106.8 %while.25 = (s32[]{:T(128)}, f32[4352,1,128]{2,0,1:T(8,128)}, f32[4352,1,128]{2,0,1:T(8,128)}, f32[8,512,1,128]{3,1,0,2:T(8,128)}, s32[8]{0:T(128)S(1)}, /*index...) while((s32[]{:T(128)}, f32[4352,1,128]{2,0,1:T(8,128)}, ...), condition=%wide.region_21.22_spmd, body=%wide.region_17.21_spmd.sunk | while | flops 510753280 | bytes 23696676 | solution.py:125
  582.2 3.1 copy.112
  585.3 3.1 multiply_reduce_fusion
  589.0 3.3 multiply_convert_fusion
  592.3 7.0 all-to-all-start.5
  603.8 17.2 %all-to-all-done.5 = bf16[32,128,128]{1,2,0:T(8,128)(2,1)S(1)} async-done(((bf16[32,128,128]{1,2,0:T(8,128)(2,1)}), bf16[32,128,128]{1,2,0:T(8,128)(2,1)S(1)}, u32[]{:S(2)}, u32[]{:S(2)}) %all-to-all-start.5) | async-done | bytes 1048608 | tf_op jit(solution)/shard_map/all_to_all | solution.py:220
  622.0 7.2 all-to-all-start.6
  635.2 38.2 %all-to-all-done.6 = f32[32,128,128]{1,2,0:T(8,128)S(1)} async-done(((f32[32,128,128]{1,2,0:T(8,128)}), f32[32,128,128]{1,2,0:T(8,128)S(1)}, u32[]{:S(2)}, u32[]{:S(2)}) %all-to-all-start.6) | async-done | bytes 2097184 | tf_op jit(solution)/shard_map/all_to_all | solution.py:228
  673.4 8.6 %all-to-all-start.7 = ((f32[32,128,128]{1,2,0:T(8,128)}), f32[32,128,128]{1,2,0:T(8,128)}, u32[]{:S(2)}, u32[]{:S(2)}) async-start(f32[32,128,128]{1,2,0:T(8,128)} %copy.121), calls=%async_computation.7 | async-start | bytes 4194304 | tf_op jit(solution)/shard_map/all_to_all | solution.py:235
  686.2 40.4 %all-to-all-done.7 = f32[32,128,128]{1,2,0:T(8,128)} async-done(((f32[32,128,128]{1,2,0:T(8,128)}), f32[32,128,128]{1,2,0:T(8,128)}, u32[]{:S(2)}, u32[]{:S(2)}) %all-to-all-start.7) | async-done | bytes 2097184 | tf_op jit(solution)/shard_map/all_to_all | solution.py:235
  729.5 102.0 %all-reduce.7 = (f32[128]{0:T(128)}, f32[128]{0:T(128)}) all-reduce(f32[128]{0:T(128)S(1)} %copy-done.19, f32[128]{0:T(128)S(1)} %bitcast_reduce_fusion.2), channel_id=1, replica_groups=mesh['dp'=16,'ctx'=32] {'dp','ctx'}, use_global_device_ids=true, to_apply=%region_27.28 | all-reduce | flops 256 | bytes 2048 | tf_op jit(solution)/shard_map/psum | solution.py:246
  (331 shorter events, 190.3 us)
Async XLA Ops:
  8.2 15.0 %copy-start.9 = (bf16[1,128,1024]{2,1,0:T(8,128)(2,1)S(1)}, bf16[1,128,1024]{2,1,0:T(8,128)(2,1)}, u32[]{:S(2)}) copy-start(bf16[1,128,1024]{2,1,0:T(8,128)(2,1)} %param.12) | copy-start | bytes 786436
  8.2 16.0 %copy-start.13 = (f32[128]{0:T(128)S(1)}, f32[128]{0:T(128)}, u32[]{:S(2)}) copy-start(f32[128]{0:T(128)} %param.17) | copy-start | bytes 1540
  9.4 39.9 %all-to-all-start = ((bf16[128,32,128]{2,0,1:T(8,128)(2,1)}), bf16[128,32,128]{2,0,1:T(8,128)(2,1)S(1)}, u32[]{:S(2)}, u32[]{:S(2)}) async-start(bf16[128,32,128]{2,0,1:T(8,128)(2,1)} %bitcast.29), calls=%async_computation | async-start | bytes 2097152 | tf_op jit(solution)/shard_map/all_to_all | solution.py:197
  23.4 27.1 %copy-start.10 = (f32[128,8]{0,1:T(8,128)}, f32[128,8]{0,1:T(8,128)S(1)}, u32[]{:S(2)}) copy-start(f32[128,8]{0,1:T(8,128)S(1)} %add_rsqrt_fusion.1) | copy-start | bytes 12292
  50.6 31.6 %all-to-all-start.1 = ((bf16[128,32,128]{2,0,1:T(8,128)(2,1)}), bf16[128,32,128]{2,0,1:T(8,128)(2,1)S(1)}, u32[]{:S(2)}, u32[]{:S(2)}) async-start(bf16[128,32,128]{2,0,1:T(8,128)(2,1)} %bitcast.33), calls=%async_computation.1 | async-start | bytes 2097152 | tf_op jit(solution)/shard_map/all_to_all | solution.py:196
  57.0 32.1 %copy-start.17 = (s32[1,128]{1,0:T(1,128)S(1)}, s32[1,128]{1,0:T(1,128)}, u32[]{:S(2)}) copy-start(s32[1,128]{1,0:T(1,128)} %param.14) | copy-start | bytes 1540
  82.2 31.2 %all-to-all-start.2 = ((bf16[128,32,128]{0,2,1:T(8,128)(2,1)}), bf16[128,32,128]{0,2,1:T(8,128)(2,1)S(1)}, u32[]{:S(2)}, u32[]{:S(2)}) async-start(bf16[128,32,128]{0,2,1:T(8,128)(2,1)} %bitcast.243), calls=%async_computation.2 | async-start | bytes 2097152 | tf_op jit(solution)/shard_map/all_to_all | solution.py:195
  113.5 3.6 copy-start.3
  160.9 32.3 %all-to-all-start.3 = ((bf16[32,128,128]{2,1,0:T(8,128)(2,1)}), bf16[32,128,128]{2,1,0:T(8,128)(2,1)S(1)}, u32[]{:S(2)}, u32[]{:S(2)}) async-start(bf16[32,128,128]{2,1,0:T(8,128)(2,1)} %bitcast.247), calls=%async_computation.3 | async-start | bytes 2097152 | tf_op jit(solution)/shard_map/all_to_all | solution.py:213
  168.3 189.7 %all-reduce.10.cloned.1.call-start = ((), (), s32[]{:S(2)}) async-start(), calls=%async_computation.9 | async-start | bytes 4194304
  193.8 3.9 copy-start.18
  193.8 164.2 %copy-start.8 = (f32[1,4,4096]{2,1,0:T(4,128)S(1)}, f32[1,4,4096]{2,1,0:T(4,128)}, u32[]{:S(2)}) copy-start(f32[1,4,4096]{2,1,0:T(4,128)} %param.15) | copy-start | bytes 196612
  195.6 245.3 %all-gather.3.cloned.1.call-start = ((), (), s32[]{:S(2)}) async-start(), calls=%async_computation.8 | async-start | bytes 1081344 | tf_op jit(solution)/shard_map/all_gather | solution.py:162
  444.8 27.6 %all-to-all-start.4 = ((bf16[128,32,128]{2,0,1:T(8,128)(2,1)}), bf16[128,32,128]{2,0,1:T(8,128)(2,1)}, u32[]{:S(2)}, u32[]{:S(2)}) async-start(bf16[128,32,128]{2,0,1:T(8,128)(2,1)} %fusion.42), calls=%async_computation.4 | async-start | bytes 2097152 | tf_op jit(solution)/shard_map/all_to_all | solution.py:217
  582.2 3.1 copy-start.1
  582.2 3.1 copy-start.12
  582.2 3.1 copy-start.16
  585.3 3.8 copy-start.4
  589.0 10.3 %copy-start.2 = (f32[4352,1,128]{2,0,1:T(8,128)S(1)}, f32[4352,1,128]{2,0,1:T(8,128)}, u32[]{:S(2)}) copy-start(f32[4352,1,128]{2,0,1:T(8,128)} %get-tuple-element.111) | copy-start | bytes 6684676
  592.3 28.6 %all-to-all-start.5 = ((bf16[32,128,128]{1,2,0:T(8,128)(2,1)}), bf16[32,128,128]{1,2,0:T(8,128)(2,1)S(1)}, u32[]{:S(2)}, u32[]{:S(2)}) async-start(bf16[32,128,128]{1,2,0:T(8,128)(2,1)} %multiply_convert_fusion), calls=%async_computation.5 | async-start | bytes 2097152 | tf_op jit(solution)/shard_map/all_to_all | solution.py:220
  622.0 51.4 %all-to-all-start.6 = ((f32[32,128,128]{1,2,0:T(8,128)}), f32[32,128,128]{1,2,0:T(8,128)S(1)}, u32[]{:S(2)}, u32[]{:S(2)}) async-start(f32[32,128,128]{1,2,0:T(8,128)} %copy.117), calls=%async_computation.6 | async-start | bytes 4194304 | tf_op jit(solution)/shard_map/all_to_all | solution.py:228
  635.1 46.8 %copy-start.14 = (f32[128]{0:T(128)S(1)}, f32[128]{0:T(128)}, u32[]{:S(2)}) copy-start(f32[128]{0:T(128)} %param.17) | copy-start | bytes 1540
  673.4 53.3 %all-to-all-start.7 = ((f32[32,128,128]{1,2,0:T(8,128)}), f32[32,128,128]{1,2,0:T(8,128)}, u32[]{:S(2)}, u32[]{:S(2)}) async-start(f32[32,128,128]{1,2,0:T(8,128)} %copy.121), calls=%async_computation.7 | async-start | bytes 4194304 | tf_op jit(solution)/shard_map/all_to_all | solution.py:235
  686.2 43.3 %copy-start.19 = (f32[128]{0:T(128)S(1)}, f32[128]{0:T(128)}, u32[]{:S(2)}) copy-start(f32[128]{0:T(128)} %get-tuple-element.153) | copy-start | bytes 1540
  (6 other events, 10.9 us)
Sparse Core Ops, SparseCore 0:
  195.8 162.1 all-reduce.9
  362.2 78.6 all-gather.2
where the time goes:
time: 841 us; the launch traced here: 838 us
  waiting for transfers between devices  447 us (53%)
  blocking collectives  102 us (12%)
  local copies, waits for them, and re-layouts  92.7 us (11%)
  matrix products  77.2 us (9%)
  starting transfers between devices  63.1 us (8%)
  other arithmetic  29.8 us (4%)
  between operations  15.2 us (2%)
  loops' own time  11.5 us (1%)
    unnamed x3, waiting for transfers between devices  160 us
    psum x1, blocking collectives, body(): total_qgain, total_kgain = lax.psum((grad_qgain, grad_kgain), ('dp', 'ctx'))  102 us
    all_gather x1, waiting for transfers between devices, spread_tokens(): lax.all_gather(scaled.astype(jnp.bfloat16), 'ctx', axis=0, tiled=True)  79.2 us
    all_to_all x1, waiting for transfers between devices, body(): lax.all_to_all(grad_head_v.reshape(total, local_heads * width), 'ctx', sp...  40.4 us
    all_to_all x1, waiting for transfers between devices, body(): lax.all_to_all(grad_head_k.reshape(total, local_heads * width), 'ctx', sp...  38.2 us
    all_to_all x1, waiting for transfers between devices, body(): lax.all_to_all(value_rep, 'ctx', split_axis=1, concat_axis=0, tiled=True)  24.6 us
    all_to_all x1, waiting for transfers between devices, body(): lax.all_to_all(attended, 'ctx', split_axis=0, concat_axis=1, tiled=True)  24.6 us
    all_to_all x1, waiting for transfers between devices, body(): lax.all_to_all(key_rep, 'ctx', split_axis=1, concat_axis=0, tiled=True)  23 us
  transfers between devices with their start and end apart: 10, of which 10 were waited for; matrix products, arithmetic and copies ran while one was open for 3% of the time, Pallas kernels for 0%

commit v1 on v0

--- a/solution.py
+++ b/solution.py
@@ -159,9 +159,12 @@
 
 
 def spread_tokens(scaled, token_ids):
-    whole = lax.all_gather(scaled.astype(jnp.bfloat16), "ctx", axis=0, tiled=True).astype(
-        scaled.dtype
-    )
+    whole = jnp.concatenate(
+        lax.all_to_all(
+            jnp.stack([scaled.astype(jnp.bfloat16)] * lax.axis_size("ctx")), "ctx", 0, 0
+        ),
+        axis=0,
+    ).astype(scaled.dtype)
     return jnp.take(whole, token_ids, axis=0).astype(jnp.bfloat16)
 
 

time: 841 us -> 800 us (0.951)
  waiting for transfers between devices: 447 us -> 392 us
  starting transfers between devices: 63.1 us -> 71.8 us
    all_gather x1 -> x0, waiting for transfers between devices: 79.2 us -> none  [spread_tokens(): lax.all_gather(scaled.astype(jnp.bfloat16), 'ctx', axis=0, tiled=True)]
    all_to_all x0 -> x1, waiting for transfers between devices: none -> 21.8 us  [spread_tokens(): lax.all_to_all(jnp.stack([scaled.astype(jnp.bfloat16)] * lax.axis_size('c...]
    unnamed x3 -> x2, waiting for transfers between devices: 160 us -> 160 us
where the time goes in v1:
time: 800 us; the launch traced here: 797 us
  waiting for transfers between devices  392 us (49%)
  blocking collectives  101 us (13%)
  local copies, waits for them, and re-layouts  98.5 us (12%)
  matrix products  77.2 us (10%)
  starting transfers between devices  71.8 us (9%)
  other arithmetic  29.8 us (4%)
  between operations  15.2 us (2%)
  loops' own time  11.5 us (1%)
    unnamed x2, waiting for transfers between devices  160 us
    psum x1, blocking collectives, body(): total_qgain, total_kgain = lax.psum((grad_qgain, grad_kgain), ('dp', 'ctx'))  101 us
    all_to_all x1, waiting for transfers between devices, body(): lax.all_to_all(grad_head_v.reshape(total, local_heads * width), 'ctx', sp...  41.4 us
    all_to_all x1, waiting for transfers between devices, body(): lax.all_to_all(grad_head_k.reshape(total, local_heads * width), 'ctx', sp...  38.7 us
    all_to_all x1, waiting for transfers between devices, body(): lax.all_to_all(value_rep, 'ctx', split_axis=1, concat_axis=0, tiled=True)  24.6 us
    all_to_all x1, waiting for transfers between devices, body(): lax.all_to_all(attended, 'ctx', split_axis=0, concat_axis=1, tiled=True)  24.6 us
    all_to_all x1, waiting for transfers between devices, body(): lax.all_to_all(key_rep, 'ctx', split_axis=1, concat_axis=0, tiled=True)  23 us
    dot_general x16, matrix products, block_probs(): jnp.einsum('rgpe,kge->gprk', grouped, keys, preferred_element_type=jnp.fl...  22.2 us
  transfers between devices with their start and end apart: 10, of which 10 were waited for; matrix products, arithmetic and copies ran while one was open for 3% of the time, Pallas kernels for 0%

profile of v1, /device:TPU:1, one launch (start us, length us, event | category | flops | bytes accessed | tf_op | source)
XLA Modules:
  0.0 796.9 jit_solution(9833089151682916428)
XLA Ops:
  9.4 13.7 %all-to-all-start = ((bf16[128,32,128]{2,0,1:T(8,128)(2,1)}), bf16[128,32,128]{2,0,1:T(8,128)(2,1)S(1)}, u32[]{:S(2)}, u32[]{:S(2)}) async-start(bf16[128,32,128]{2,0,1:T(8,128)(2,1)} %bitcast.29), calls=%async_computation | async-start | bytes 2097152 | tf_op jit(solution)/shard_map/all_to_all | solution.py:200
  24.8 24.6 %all-to-all-done = bf16[128,32,128]{2,0,1:T(8,128)(2,1)S(1)} async-done(((bf16[128,32,128]{2,0,1:T(8,128)(2,1)}), bf16[128,32,128]{2,0,1:T(8,128)(2,1)S(1)}, u32[]{:S(2)}, u32[]{:S(2)}) %all-to-all-start) | async-done | bytes 1048608 | tf_op jit(solution)/shard_map/all_to_all | solution.py:200
  50.6 6.4 all-to-all-start.1
  59.3 23.0 %all-to-all-done.1 = bf16[128,32,128]{2,0,1:T(8,128)(2,1)S(1)} async-done(((bf16[128,32,128]{2,0,1:T(8,128)(2,1)}), bf16[128,32,128]{2,0,1:T(8,128)(2,1)S(1)}, u32[]{:S(2)}, u32[]{:S(2)}) %all-to-all-start.1) | async-done | bytes 1048608 | tf_op jit(solution)/shard_map/all_to_all | solution.py:199
  82.2 6.8 all-to-all-start.2
  95.0 18.5 %all-to-all-done.2 = bf16[128,32,128]{0,2,1:T(8,128)(2,1)S(1)} async-done(((bf16[128,32,128]{0,2,1:T(8,128)(2,1)}), bf16[128,32,128]{0,2,1:T(8,128)(2,1)S(1)}, u32[]{:S(2)}, u32[]{:S(2)}) %all-to-all-start.2) | async-done | bytes 1048608 | tf_op jit(solution)/shard_map/all_to_all | solution.py:198
  119.0 41.8 %while.24 = (s32[]{:T(128)}, bf16[8,512,128]{2,1,0:T(8,128)(2,1)}, s32[8]{0:T(128)S(1)}, bf16[4352,1,128]{2,0,1:T(8,128)(2,1)}, s32[4096]{0:T(1024)S(1)}, /*inde...) while((s32[]{:T(128)}, bf16[8,512,128]{2,1,0:T(8,128)(2,1)}, ...), condition=%wide.region_9.10_spmd, body=%wide.region_6.9_spmd.sunk | while | flops 204930048 | bytes 5924080 | solution.py:96
  160.8 7.4 all-to-all-start.3
  168.5 24.6 %all-to-all-done.3 = bf16[32,128,128]{2,1,0:T(8,128)(2,1)S(1)} async-done(((bf16[32,128,128]{2,1,0:T(8,128)(2,1)}), bf16[32,128,128]{2,1,0:T(8,128)(2,1)S(1)}, u32[]{:S(2)}, u32[]{:S(2)}) %all-to-all-start.3) | async-done | bytes 1048608 | tf_op jit(solution)/shard_map/all_to_all | solution.py:216
  197.7 160.3 %all-reduce.10.cloned.1.call-done = f32[128,4096]{1,0:T(8,128)} async-done(((f32[128,4096]{1,0:T(8,128)}), f32[128,4096]{1,0:T(8,128)}) %all-reduce.10.cloned.1.call-update) | async-done | bytes 2097168
  363.1 5.5 all-to-all-start.4
  368.6 21.8 %all-to-all-done.4 = bf16[32,4,4096]{2,1,0:T(4,128)(2,1)S(1)} async-done(((bf16[32,4,4096]{2,1,0:T(4,128)(2,1)}), bf16[32,4,4096]{2,1,0:T(4,128)(2,1)S(1)}, u32[]{:S(2)}, u32[]{:S(2)}) %all-to-all-start.4) | async-done | bytes 1048608 | tf_op jit(solution)/shard_map/all_to_all | solution.py:163
  393.2 8.3 %all-to-all-start.5 = ((bf16[128,32,128]{2,0,1:T(8,128)(2,1)}), bf16[128,32,128]{2,0,1:T(8,128)(2,1)}, u32[]{:S(2)}, u32[]{:S(2)}) async-start(bf16[128,32,128]{2,0,1:T(8,128)(2,1)} %fusion.42), calls=%async_computation.5 | async-start | bytes 2097152 | tf_op jit(solution)/shard_map/all_to_all | solution.py:220
  402.1 21.4 %all-to-all-done.5 = bf16[128,32,128]{2,0,1:T(8,128)(2,1)} async-done(((bf16[128,32,128]{2,0,1:T(8,128)(2,1)}), bf16[128,32,128]{2,0,1:T(8,128)(2,1)}, u32[]{:S(2)}, u32[]{:S(2)}) %all-to-all-start.5) | async-done | bytes 1048608 | tf_op jit(solution)/shard_map/all_to_all | solution.py:220
  426.6 112.2 %while.25 = (s32[]{:T(128)}, f32[4352,1,128]{2,0,1:T(8,128)}, f32[4352,1,128]{2,0,1:T(8,128)}, f32[8,512,1,128]{3,1,0,2:T(8,128)}, s32[8]{0:T(128)S(1)}, /*index...) while((s32[]{:T(128)}, f32[4352,1,128]{2,0,1:T(8,128)}, ...), condition=%wide.region_21.22_spmd, body=%wide.region_17.21_spmd.sunk | while | flops 510753280 | bytes 23696676 | solution.py:125
  541.9 3.1 multiply_reduce_fusion
  545.7 3.3 multiply_convert_fusion
  548.9 7.6 all-to-all-start.6
  561.0 17.7 %all-to-all-done.6 = bf16[32,128,128]{1,2,0:T(8,128)(2,1)S(1)} async-done(((bf16[32,128,128]{1,2,0:T(8,128)(2,1)}), bf16[32,128,128]{1,2,0:T(8,128)(2,1)S(1)}, u32[]{:S(2)}, u32[]{:S(2)}) %all-to-all-start.6) | async-done | bytes 1048608 | tf_op jit(solution)/shard_map/all_to_all | solution.py:223
  579.7 7.8 all-to-all-start.7
  593.5 38.7 %all-to-all-done.7 = f32[32,128,128]{1,2,0:T(8,128)S(1)} async-done(((f32[32,128,128]{1,2,0:T(8,128)}), f32[32,128,128]{1,2,0:T(8,128)S(1)}, u32[]{:S(2)}, u32[]{:S(2)}) %all-to-all-start.7) | async-done | bytes 2097184 | tf_op jit(solution)/shard_map/all_to_all | solution.py:231
  632.2 8.3 %all-to-all-start.8 = ((f32[32,128,128]{1,2,0:T(8,128)}), f32[32,128,128]{1,2,0:T(8,128)}, u32[]{:S(2)}, u32[]{:S(2)}) async-start(f32[32,128,128]{1,2,0:T(8,128)} %copy.121), calls=%async_computation.8 | async-start | bytes 4194304 | tf_op jit(solution)/shard_map/all_to_all | solution.py:238
  644.9 41.4 %all-to-all-done.8 = f32[32,128,128]{1,2,0:T(8,128)} async-done(((f32[32,128,128]{1,2,0:T(8,128)}), f32[32,128,128]{1,2,0:T(8,128)}, u32[]{:S(2)}, u32[]{:S(2)}) %all-to-all-start.8) | async-done | bytes 2097184 | tf_op jit(solution)/shard_map/all_to_all | solution.py:238
  689.2 100.9 %all-reduce.7 = (f32[128]{0:T(128)}, f32[128]{0:T(128)}) all-reduce(f32[128]{0:T(128)S(1)} %copy-done.20, f32[128]{0:T(128)S(1)} %bitcast_reduce_fusion.2), channel_id=1, replica_groups=mesh['dp'=16,'ctx'=32] {'dp','ctx'}, use_global_device_ids=true, to_apply=%region_27.28 | all-reduce | flops 256 | bytes 2048 | tf_op jit(solution)/shard_map/psum | solution.py:249
  (333 shorter events, 199.1 us)
Async XLA Ops:
  8.2 15.0 %copy-start.9 = (bf16[1,128,1024]{2,1,0:T(8,128)(2,1)S(1)}, bf16[1,128,1024]{2,1,0:T(8,128)(2,1)}, u32[]{:S(2)}) copy-start(bf16[1,128,1024]{2,1,0:T(8,128)(2,1)} %param.12) | copy-start | bytes 786436
  8.2 16.0 %copy-start.14 = (f32[128]{0:T(128)S(1)}, f32[128]{0:T(128)}, u32[]{:S(2)}) copy-start(f32[128]{0:T(128)} %param.17) | copy-start | bytes 1540
  9.4 39.9 %all-to-all-start = ((bf16[128,32,128]{2,0,1:T(8,128)(2,1)}), bf16[128,32,128]{2,0,1:T(8,128)(2,1)S(1)}, u32[]{:S(2)}, u32[]{:S(2)}) async-start(bf16[128,32,128]{2,0,1:T(8,128)(2,1)} %bitcast.29), calls=%async_computation | async-start | bytes 2097152 | tf_op jit(solution)/shard_map/all_to_all | solution.py:200
  23.4 27.1 %copy-start.11 = (f32[128,8]{0,1:T(8,128)}, f32[128,8]{0,1:T(8,128)S(1)}, u32[]{:S(2)}) copy-start(f32[128,8]{0,1:T(8,128)S(1)} %add_rsqrt_fusion.1) | copy-start | bytes 12292
  50.6 31.6 %all-to-all-start.1 = ((bf16[128,32,128]{2,0,1:T(8,128)(2,1)}), bf16[128,32,128]{2,0,1:T(8,128)(2,1)S(1)}, u32[]{:S(2)}, u32[]{:S(2)}) async-start(bf16[128,32,128]{2,0,1:T(8,128)(2,1)} %bitcast.33), calls=%async_computation.1 | async-start | bytes 2097152 | tf_op jit(solution)/shard_map/all_to_all | solution.py:199
  57.0 32.1 %copy-start.18 = (s32[1,128]{1,0:T(1,128)S(1)}, s32[1,128]{1,0:T(1,128)}, u32[]{:S(2)}) copy-start(s32[1,128]{1,0:T(1,128)} %param.14) | copy-start | bytes 1540
  82.2 31.2 %all-to-all-start.2 = ((bf16[128,32,128]{0,2,1:T(8,128)(2,1)}), bf16[128,32,128]{0,2,1:T(8,128)(2,1)S(1)}, u32[]{:S(2)}, u32[]{:S(2)}) async-start(bf16[128,32,128]{0,2,1:T(8,128)(2,1)} %bitcast.241), calls=%async_computation.2 | async-start | bytes 2097152 | tf_op jit(solution)/shard_map/all_to_all | solution.py:198
  113.5 3.6 copy-start.3
  160.8 32.9 %copy-start.10 = (s32[4096]{0:T(1024)}, s32[4096]{0:T(1024)S(1)}, u32[]{:S(2)}) copy-start(s32[4096]{0:T(1024)S(1)} %get-tuple-element.473) | copy-start | bytes 49156
  160.8 32.3 %all-to-all-start.3 = ((bf16[32,128,128]{2,1,0:T(8,128)(2,1)}), bf16[32,128,128]{2,1,0:T(8,128)(2,1)S(1)}, u32[]{:S(2)}, u32[]{:S(2)}) async-start(bf16[32,128,128]{2,1,0:T(8,128)(2,1)} %bitcast.245), calls=%async_computation.3 | async-start | bytes 2097152 | tf_op jit(solution)/shard_map/all_to_all | solution.py:216
  168.3 189.7 %all-reduce.10.cloned.1.call-start = ((), (), s32[]{:S(2)}) async-start(), calls=%async_computation.9 | async-start | bytes 4194304
  193.8 3.8 copy-start.19
  193.8 164.2 %copy-start.8 = (f32[1,4,4096]{2,1,0:T(4,128)S(1)}, f32[1,4,4096]{2,1,0:T(4,128)}, u32[]{:S(2)}) copy-start(f32[1,4,4096]{2,1,0:T(4,128)} %param.15) | copy-start | bytes 196612
  363.1 27.3 %all-to-all-start.4 = ((bf16[32,4,4096]{2,1,0:T(4,128)(2,1)}), bf16[32,4,4096]{2,1,0:T(4,128)(2,1)S(1)}, u32[]{:S(2)}, u32[]{:S(2)}) async-start(bf16[32,4,4096]{2,1,0:T(4,128)(2,1)} %stack.2), calls=%async_computation.4 | async-start | bytes 2097152 | tf_op jit(solution)/shard_map/all_to_all | solution.py:163
  393.2 30.3 %all-to-all-start.5 = ((bf16[128,32,128]{2,0,1:T(8,128)(2,1)}), bf16[128,32,128]{2,0,1:T(8,128)(2,1)}, u32[]{:S(2)}, u32[]{:S(2)}) async-start(bf16[128,32,128]{2,0,1:T(8,128)(2,1)} %fusion.42), calls=%async_computation.5 | async-start | bytes 2097152 | tf_op jit(solution)/shard_map/all_to_all | solution.py:220
  538.8 3.1 copy-start.13
  538.8 3.1 copy-start.17
  541.9 3.8 copy-start.4
  545.7 10.9 %copy-start.2 = (f32[4352,1,128]{2,0,1:T(8,128)S(1)}, f32[4352,1,128]{2,0,1:T(8,128)}, u32[]{:S(2)}) copy-start(f32[4352,1,128]{2,0,1:T(8,128)} %get-tuple-element.111) | copy-start | bytes 6684676
  548.9 29.8 %all-to-all-start.6 = ((bf16[32,128,128]{1,2,0:T(8,128)(2,1)}), bf16[32,128,128]{1,2,0:T(8,128)(2,1)S(1)}, u32[]{:S(2)}, u32[]{:S(2)}) async-start(bf16[32,128,128]{1,2,0:T(8,128)(2,1)} %multiply_convert_fusion), calls=%async_computation.6 | async-start | bytes 2097152 | tf_op jit(solution)/shard_map/all_to_all | solution.py:223
  579.7 52.5 %all-to-all-start.7 = ((f32[32,128,128]{1,2,0:T(8,128)}), f32[32,128,128]{1,2,0:T(8,128)S(1)}, u32[]{:S(2)}, u32[]{:S(2)}) async-start(f32[32,128,128]{1,2,0:T(8,128)} %copy.117), calls=%async_computation.7 | async-start | bytes 4194304 | tf_op jit(solution)/shard_map/all_to_all | solution.py:231
  593.5 47.1 %copy-start.15 = (f32[128]{0:T(128)S(1)}, f32[128]{0:T(128)}, u32[]{:S(2)}) copy-start(f32[128]{0:T(128)} %param.17) | copy-start | bytes 1540
  632.2 54.1 %all-to-all-start.8 = ((f32[32,128,128]{1,2,0:T(8,128)}), f32[32,128,128]{1,2,0:T(8,128)}, u32[]{:S(2)}, u32[]{:S(2)}) async-start(f32[32,128,128]{1,2,0:T(8,128)} %copy.121), calls=%async_computation.8 | async-start | bytes 4194304 | tf_op jit(solution)/shard_map/all_to_all | solution.py:238
  644.8 44.3 %copy-start.20 = (f32[128]{0:T(128)S(1)}, f32[128]{0:T(128)}, u32[]{:S(2)}) copy-start(f32[128]{0:T(128)} %get-tuple-element.153) | copy-start | bytes 1540
  (7 other events, 14.0 us)
Sparse Core Ops, SparseCore 0:
  195.8 162.1 all-reduce.9
